TPU v7x, 32 devices: a whole 2x2x4 slice. The times are simulated.
32 devices in a mesh: groups: 2 (over x), seq: 16 (over z, y, core).
Axes of the slice: x: 2, y: 2, z: 4, core: 2. Of those that a mesh axis runs over, the one named last changes fastest.
Arguments:
- prefill_q: bfloat16 [32, 8192], P(('groups', 'seq')), parts along dimension 0, may hold values from -48 to 48
- cache_k: bfloat16 [16384, 1024], P(('groups', 'seq')), parts along dimension 0, may hold values from -4.5 to 4.5
- cache_v: bfloat16 [16384, 1024], P(('groups', 'seq')), parts along dimension 0, may hold values from -4.5 to 4.5
- page_counts: int32 [32], P('groups'), parts along dimension 0, may hold values from 1 to 64, 768 in all
- page_owner: int32 [2048, 1], P(('groups', 'seq')), parts along dimension 0, may hold values from 0 to 15; in each aligned block of 64 rows (0 to 63, 64 to 127, ...) at most 8 rows name the same one
- decode_q: bfloat16 [32, 2, 8192], P(('groups', 'seq')), parts along dimension 0, may hold values from -48 to 48
- decode_k: bfloat16 [32, 2, 1024], P(('groups', 'seq')), parts along dimension 0, may hold values from -12 to 12
- decode_v: bfloat16 [32, 2, 1024], P(('groups', 'seq')), parts along dimension 0, may hold values from -4.5 to 4.5
- context_len: int32 [32], P(('groups', 'seq')), parts along dimension 0, may hold values from 768 to 6144
Outputs:
- prefill_out: bfloat16 [32, 8192], P(('groups', 'seq')), parts along dimension 0
- decode_out: bfloat16 [32, 2, 8192], P(('groups', 'seq')), parts along dimension 0
- store_k: bfloat16 [32768, 1024], P(('groups', 'seq')), parts along dimension 0
- store_v: bfloat16 [32768, 1024], P(('groups', 'seq')), parts along dimension 0
- store_page: int32 [4096], P(('groups', 'seq')), parts along dimension 0
There are 2 independent parts, one for each index of `groups`. A program takes and returns all parts, laid end to end along the dimension named above; each array names one. Nothing has to cross between parts.
Inputs may be any that keep to these rules, and one draw needn't show every extreme that they name: `page_counts`: the counts sum to 768 and the largest equals 64. `page_owner`: within the 64 page slots of one shard each owner is named at most 8 times, and exactly 8 times in some shards.
All inputs are finite; a program needn't handle non-finite values.
Results may differ from a plain program's by a relative error of at most 0.014.
Values may be sent and summed in bfloat16 or wider, within the bound.
A program may use at most 128 MiB of HBM per device.

v0:
```python
import functools

import jax
import jax.numpy as jnp
from jax import lax
from jax.experimental import pallas as pl
from jax.experimental.pallas import tpu as pltpu
from jax.sharding import PartitionSpec as P

HQ = 64
KVH = 8
HD = 128
PAGE = 8
STEPS = 2
KVD = 1024
GROUP = HQ // KVH
ROWS = (1 + STEPS) * GROUP
LANES = 128
ID_LANE = 64
MASKED = -1e30
SCALE = HD ** (-0.5)
MESH = pl.DeviceIdType.MESH

META, KEYS, VALUES = range(3)
QROW, PART, STAT = range(3)


def pack_kernel(
    n, cap, page_slots, owner, counts, context, ck_hbm, cv_hbm, out_k, out_v, meta,
    ck, cv, table, seen, done,
):
    me = lax.axis_index("seq")
    loads = [
        pltpu.make_async_copy(ck_hbm, ck, done.at[0]),
        pltpu.make_async_copy(cv_hbm, cv, done.at[1]),
    ]
    for load in loads:
        load.start()

    def clear(i, _):
        seen[i] = 0
        for k in range(cap):
            table[i * cap + k] = -1
        return 0

    lax.fori_loop(0, n, clear, 0)

    def place(j, _):
        o = owner[j]
        k = seen[o]
        seen[o] = k + 1
        table[o * cap + k] = j
        return 0

    lax.fori_loop(0, counts[me], place, 0)

    for load in loads:
        load.wait()

    tile_row = lax.broadcasted_iota(jnp.int32, (8, LANES), 0)
    lane = lax.broadcasted_iota(jnp.int32, (8, LANES), 1)

    def fill(dst, _):
        ids = jnp.full((8, LANES), -1, jnp.int32)
        for k in range(cap):
            slot = dst * cap + k
            src = table[slot]
            page = jnp.maximum(src, 0)
            there = jnp.full((PAGE, KVD), src, jnp.int32) >= 0
            out_k[slot] = jnp.where(there, ck[page], jnp.zeros((), out_k.dtype))
            out_v[slot] = jnp.where(there, cv[page], jnp.zeros((), out_v.dtype))
            ids = jnp.where(tile_row == k, jnp.where(src >= 0, me * page_slots + src, -1), ids)
        meta[dst] = jnp.where(lane < ID_LANE, context[0], ids)
        return 0

    lax.fori_loop(0, n, fill, 0)


def pack(n, cap, owner, counts, context, ck, cv):
    page_slots = ck.shape[0]
    smem = pl.BlockSpec(memory_space=pltpu.SMEM)
    vmem = pl.BlockSpec(memory_space=pltpu.VMEM)
    hbm = pl.BlockSpec(memory_space=pl.ANY)
    return pl.pallas_call(
        functools.partial(pack_kernel, n, cap, page_slots),
        in_specs=[smem, smem, smem, hbm, hbm],
        out_specs=(vmem, vmem, vmem),
        out_shape=(
            jax.ShapeDtypeStruct((n * cap, PAGE, KVD), ck.dtype),
            jax.ShapeDtypeStruct((n * cap, PAGE, KVD), cv.dtype),
            jax.ShapeDtypeStruct((n, 8, LANES), jnp.int32),
        ),
        scratch_shapes=[
            pltpu.VMEM(ck.shape, ck.dtype), pltpu.VMEM(cv.shape, cv.dtype),
            pltpu.SMEM((n * cap,), jnp.int32), pltpu.SMEM((n,), jnp.int32),
            pltpu.SemaphoreType.DMA((2,)),
        ],
        compiler_params=pltpu.CompilerParams(vmem_limit_bytes=16 << 20),
        name="pack",
    )(owner, counts, context, ck, cv)


def main_kernel(
    n, cap, chunk, counts, q_ref, meta_ref, ck_ref, cv_ref, pk_ref, pv_ref, ok_ref, ov_ref,
    out_ref, store_k, store_v, meta_out,
    qbuf, obuf, stat, limit, got1, got1s, obuf1, stat1, got2, got2s, obuf2, stat2, pbuf, sbuf,
    page_send, page_recv, row_send, row_recv, pair_send, pair_recv, local,
):
    depth = n // 4
    me = lax.axis_index("seq")
    my_z, my_y, my_c = me // 4, (me // 2) % 2, me % 2
    block = (my_c * 2 + my_y) * depth + my_z
    across = my_z * 4 + (1 - my_y) * 2 + my_c
    sibling = my_z * 4 + my_y * 2 + (1 - my_c)

    def rows_of(first, count=1):
        return pl.ds(pl.multiple_of(first * ROWS, 8), count * ROWS)

    def slots_of(d):
        return pl.ds(d * cap, cap)

    def page_ends(kind, peer, writer):
        if kind == META:
            return meta_ref.at[peer], meta_out.at[writer]
        if kind == KEYS:
            return pk_ref.at[slots_of(peer)], store_k.at[slots_of(writer)]
        return pv_ref.at[slots_of(peer)], store_v.at[slots_of(writer)]

    def page(kind, peer, arriving=False):
        src, dst = page_ends(kind, peer, peer if arriving else me)
        return pltpu.make_async_remote_copy(
            src_ref=src, dst_ref=dst, send_sem=page_send.at[kind, peer],
            recv_sem=page_recv.at[kind, peer if arriving else me],
            device_id={"seq": peer}, device_id_type=MESH,
        )

    def row_ends(kind, z, writer):
        if kind == QROW:
            return q_ref, qbuf.at[:, rows_of((my_c * 2 + my_y) * depth + writer), :]
        if kind == PART:
            return obuf2.at[:, rows_of(z), :], pbuf.at[writer]
        return stat2.at[rows_of(z), :], sbuf.at[writer]

    def row(kind, z, arriving=False):
        src, dst = row_ends(kind, z, z if arriving else my_z)
        return pltpu.make_async_remote_copy(
            src_ref=src, dst_ref=dst, send_sem=row_send.at[kind, z],
            recv_sem=row_recv.at[kind, z if arriving else my_z],
            device_id={"seq": z * 4 + my_y * 2 + my_c}, device_id_type=MESH,
        )

    def pair(number, src, dst, peer):
        return pltpu.make_async_remote_copy(
            src_ref=src, dst_ref=dst, send_sem=pair_send.at[number], recv_sem=pair_recv.at[number],
            device_id={"seq": peer}, device_id_type=MESH,
        )

    def own_page(kind):
        src, dst = page_ends(kind, me, me)
        return pltpu.make_async_copy(src, dst, local.at[kind])

    def own_row(kind):
        src, dst = row_ends(kind, my_z, my_z)
        return pltpu.make_async_copy(src, dst, local.at[3 + kind])

    def each(count, mine, body):
        def step(i, _):
            body(lax.rem(mine + i, count))
            return 0

        lax.fori_loop(1, count, step, 0)

    barrier = pltpu.get_barrier_semaphore()

    def greet(peer):
        pl.semaphore_signal(barrier, inc=1, device_id={"seq": peer}, device_id_type=MESH)

    each(n, me, greet)
    pl.semaphore_wait(barrier, n - 1)

    each(depth, my_z, lambda z: row(QROW, z).start())
    own_row(QROW).start()
    each(n, me, lambda peer: page(META, peer).start())
    for kind in (META, KEYS, VALUES):
        own_page(kind).start()

    def start_pages(peer):
        page(KEYS, peer).start()
        page(VALUES, peer).start()

    def near(i, _):
        z = lax.rem(my_z + depth // 2 + i, depth)

        @pl.when(z != my_z)
        def _():
            start_pages(z * 4 + my_y * 2 + my_c)
            start_pages(z * 4 + my_y * 2 + (1 - my_c))

        return 0

    lax.fori_loop(0, depth, near, 0)

    own_row(QROW).wait()
    each(depth, my_z, lambda z: row(QROW, z, True).wait_recv())
    q_y_out = qbuf.at[:, rows_of((my_c * 2 + my_y) * depth, depth), :]
    q_y_in = qbuf.at[:, rows_of((my_c * 2 + 1 - my_y) * depth, depth), :]
    pair(0, q_y_out, q_y_out, across).start()
    pair(0, q_y_out, q_y_in, across).wait_recv()
    q_c_out = qbuf.at[:, rows_of(my_c * 2 * depth, 2 * depth), :]
    q_c_in = qbuf.at[:, rows_of((1 - my_c) * 2 * depth, 2 * depth), :]
    pair(1, q_c_out, q_c_out, sibling).start()
    own_page(META).wait()
    each(n, me, lambda peer: page(META, peer, True).wait_recv())

    live = PAGE * counts[me]
    start = PAGE * lax.fori_loop(
        0, n, lambda i, sofar: sofar + jnp.where(i < me, counts[i], 0), jnp.int32(0)
    )
    prompt = PAGE * lax.fori_loop(0, n, lambda i, sofar: sofar + counts[i], jnp.int32(0))

    def set_limit(p, _):
        d = (p % depth) * 4 + ((p // depth) % 2) * 2 + p // (2 * depth)
        base = pl.multiple_of(p * ROWS, 8)
        context = jnp.broadcast_to(meta_out[d][:, 0:1], (8, LANES))
        reach = jnp.minimum(live, context - start)
        limit[pl.ds(base, 8), :] = jnp.full(
            (8, LANES), jnp.minimum(live, prompt - n + d + 1 - start)
        )
        for s in range(STEPS):
            limit[pl.ds(pl.multiple_of(base + 8 * (s + 1), 8), 8), :] = reach
        return 0

    lax.fori_loop(0, n, set_limit, 0)
    pair(1, q_c_out, q_c_in, sibling).wait_recv()

    def far(i, _):
        z = lax.rem(my_z + depth // 2 + i, depth)
        start_pages(z * 4 + (1 - my_y) * 2 + my_c)
        start_pages(z * 4 + (1 - my_y) * 2 + (1 - my_c))
        return 0

    far(0, 0)

    lane = lax.broadcasted_iota(jnp.int32, (chunk, LANES), 1)
    keys = ck_ref.shape[0]

    def attend(c, _):
        rows = pl.ds(pl.multiple_of(c * chunk, 16), chunk)

        def head(g, stats):
            cols = pl.ds(pl.multiple_of(g * HD, HD), HD)
            scores = lax.dot_general(
                qbuf[g, rows, :], ck_ref[:, cols], (((1,), (1,)), ((), ())),
                preferred_element_type=jnp.float32,
            ) * SCALE
            place = lax.broadcasted_iota(jnp.int32, (chunk, keys), 1)
            bound = limit[rows, 0:1]
            scores = jnp.where(place < bound, scores, MASKED)
            high = jnp.max(scores, axis=1, keepdims=True)
            weights = jnp.exp(scores - high)
            total = jnp.sum(weights, axis=1, keepdims=True)
            summed = jnp.dot(
                weights.astype(jnp.bfloat16), cv_ref[:, cols], preferred_element_type=jnp.float32
            )
            obuf[g, rows, :] = (summed / total).astype(jnp.bfloat16)
            level = jnp.where(bound > 0, high + jnp.log(total), MASKED)
            return jnp.where(lane == g, level, stats)

        stat[rows, :] = lax.fori_loop(0, KVH, head, jnp.zeros((chunk, LANES), jnp.float32))
        return 0

    lax.fori_loop(0, stat.shape[0] // chunk, attend, 0)

    def merge(a, a_stat, first, b, b_stat, to, to_stat):
        step = 2 * ROWS

        def some(i, _):
            here = pl.ds(pl.multiple_of(i * step, 16), step)
            there = pl.ds(pl.multiple_of(first * ROWS + i * step, 16), step)
            one, two = a_stat[there, :], b_stat[here, :]
            high = jnp.maximum(one, two)
            one, two = jnp.exp(one - high), jnp.exp(two - high)
            both = one + two
            to_stat[here, :] = high + jnp.log(both)
            one, two = one / both, two / both
            for g in range(KVH):
                to[g, here, :] = (
                    one[:, g : g + 1] * a[g, there, :].astype(jnp.float32)
                    + two[:, g : g + 1] * b[g, here, :].astype(jnp.float32)
                ).astype(jnp.bfloat16)
            return 0

        lax.fori_loop(0, to_stat.shape[0] // step, some, 0)

    give = (1 - my_c) * 2 * depth
    part1 = pair(2, obuf.at[:, rows_of(give, 2 * depth), :], got1, sibling)
    part1s = pair(3, stat.at[rows_of(give, 2 * depth), :], got1s, sibling)
    part1s.start()
    part1.start()
    part1s.wait_recv()
    part1.wait_recv()
    merge(obuf, stat, my_c * 2 * depth, got1, got1s, obuf1, stat1)
    give = (1 - my_y) * depth
    part2 = pair(4, obuf1.at[:, rows_of(give, depth), :], got2, across)
    part2s = pair(5, stat1.at[rows_of(give, depth), :], got2s, across)
    part2s.start()
    part2.start()
    start_pages(sibling)

    own_lane = lax.broadcasted_iota(jnp.int32, (ROWS, LANES), 1)
    own_place = lax.broadcasted_iota(jnp.int32, (ROWS, LANES), 0)
    own_levels = []
    for t in range(STEPS):
        level = jnp.zeros((ROWS, LANES), jnp.float32)
        for g in range(KVH):
            key = ok_ref[t : t + 1, g * HD : (g + 1) * HD].astype(jnp.float32)
            score = jnp.sum(q_ref[g].astype(jnp.float32) * key, axis=1, keepdims=True) * SCALE
            level = jnp.where(own_lane == g, score, level)
        own_levels.append(jnp.where(own_place >= GROUP * (t + 1), level, MASKED))

    part2s.wait_recv()
    part2.wait_recv()
    merge(obuf1, stat1, my_y * depth, got2, got2s, obuf2, stat2)

    def start_rows(z):
        row(STAT, z).start()
        row(PART, z).start()

    each(depth, my_z, start_rows)
    own_row(STAT).start()
    own_row(PART).start()

    lax.fori_loop(1, depth, far, 0)

    own_row(STAT).wait()
    own_row(PART).wait()

    def wait_rows(z):
        row(STAT, z, True).wait_recv()
        row(PART, z, True).wait_recv()

    each(depth, my_z, wait_rows)

    top = functools.reduce(jnp.maximum, own_levels)
    top = lax.fori_loop(0, depth, lambda d, high: jnp.maximum(high, sbuf[d]), top)

    norm = jnp.zeros((ROWS, LANES), jnp.float32)
    sums = [jnp.zeros((ROWS, HD), jnp.float32) for _ in range(KVH)]
    for t in range(STEPS):
        factor = jnp.exp(own_levels[t] - top)
        norm = norm + factor
        for g in range(KVH):
            value = ov_ref[t : t + 1, g * HD : (g + 1) * HD].astype(jnp.float32)
            sums[g] = sums[g] + factor[:, g : g + 1] * value

    def add(d, state):
        norm, sums = state
        factor = jnp.exp(sbuf[d] - top)
        sums = tuple(
            sums[g] + factor[:, g : g + 1] * pbuf[d, g].astype(jnp.float32) for g in range(KVH)
        )
        return norm + factor, sums

    norm, sums = lax.fori_loop(0, depth, add, (norm, tuple(sums)))
    for g in range(KVH):
        out_ref[g] = (sums[g] / norm[:, g : g + 1]).astype(out_ref.dtype)

    pair(0, q_y_out, q_y_out, across).wait_send()
    pair(1, q_c_out, q_c_out, sibling).wait_send()
    for copy in (part1, part1s, part2, part2s):
        copy.wait_send()

    def finish_row(z):
        for kind in (QROW, PART, STAT):
            row(kind, z).wait_send()

    each(depth, my_z, finish_row)
    own_page(KEYS).wait()
    own_page(VALUES).wait()

    def finish(peer):
        page(KEYS, peer, True).wait_recv()
        page(VALUES, peer, True).wait_recv()
        for kind in (META, KEYS, VALUES):
            page(kind, peer).wait_send()

    each(n, me, finish)


def main(n, cap, counts, q, meta, ck, cv, pk, pv, own_k, own_v):
    height = n * ROWS
    chunk = min(height, 384)
    vmem = pl.BlockSpec(memory_space=pltpu.VMEM)
    smem = pl.BlockSpec(memory_space=pltpu.SMEM)

    def parts(rows):
        return pltpu.VMEM((KVH, rows, HD), jnp.bfloat16)

    def stats(rows):
        return pltpu.VMEM((rows, LANES), jnp.float32)

    half, quarter, depth = height // 2, height // 4, n // 4
    return pl.pallas_call(
        functools.partial(main_kernel, n, cap, chunk),
        in_specs=[smem] + [vmem] * 8,
        out_specs=(vmem, vmem, vmem, vmem),
        out_shape=(
            jax.ShapeDtypeStruct((KVH, ROWS, HD), jnp.bfloat16),
            jax.ShapeDtypeStruct(pk.shape, pk.dtype),
            jax.ShapeDtypeStruct(pv.shape, pv.dtype),
            jax.ShapeDtypeStruct(meta.shape, meta.dtype),
        ),
        scratch_shapes=[
            parts(height), parts(height), stats(height), pltpu.VMEM((height, LANES), jnp.int32),
            parts(half), stats(half), parts(half), stats(half),
            parts(quarter), stats(quarter), parts(quarter), stats(quarter),
            pltpu.VMEM((depth, KVH, ROWS, HD), jnp.bfloat16),
            pltpu.VMEM((depth, ROWS, LANES), jnp.float32),
            pltpu.SemaphoreType.DMA((3, n)),
            pltpu.SemaphoreType.DMA((3, n)),
            pltpu.SemaphoreType.DMA((3, depth)),
            pltpu.SemaphoreType.DMA((3, depth)),
            pltpu.SemaphoreType.DMA((6,)),
            pltpu.SemaphoreType.DMA((6,)),
            pltpu.SemaphoreType.DMA((6,)),
        ],
        compiler_params=pltpu.CompilerParams(
            collective_id=0, has_side_effects=True, vmem_limit_bytes=32 << 20
        ),
        name="exchange",
    )(counts, q, meta, ck, cv, pk, pv, own_k, own_v)


def write_kernel(k_in, v_in, k_out, v_out, done):
    copies = [
        pltpu.make_async_copy(k_in, k_out, done.at[0]),
        pltpu.make_async_copy(v_in, v_out, done.at[1]),
    ]
    for copy in copies:
        copy.start()
    for copy in copies:
        copy.wait()


def write(store_k, store_v):
    vmem = pl.BlockSpec(memory_space=pltpu.VMEM)
    hbm = pl.BlockSpec(memory_space=pl.ANY)
    return pl.pallas_call(
        write_kernel,
        in_specs=[vmem, vmem],
        out_specs=(hbm, hbm),
        out_shape=(
            jax.ShapeDtypeStruct(store_k.shape, store_k.dtype),
            jax.ShapeDtypeStruct(store_v.shape, store_v.dtype),
        ),
        scratch_shapes=[pltpu.SemaphoreType.DMA((2,))],
        compiler_params=pltpu.CompilerParams(vmem_limit_bytes=16 << 20),
        name="write",
    )(store_k, store_v)


def per_device(
    prefill_q, cache_k, cache_v, page_counts, page_owner, decode_q, decode_k, decode_v, context_len
):
    n = lax.axis_size("seq")
    me = lax.axis_index("seq")
    page_slots = cache_k.shape[0] // PAGE
    cap = max(2, 2 * page_slots // n)
    ck = cache_k.reshape(page_slots, PAGE, KVD)
    cv = cache_v.reshape(page_slots, PAGE, KVD)
    pk, pv, meta = pack(n, cap, page_owner[:, 0], page_counts, context_len, ck, cv)
    q = jnp.concatenate((prefill_q, decode_q[0]), axis=0)
    q = q.reshape(1 + STEPS, KVH, GROUP, HD).transpose(1, 0, 2, 3).reshape(KVH, ROWS, HD)
    out, store_k, store_v, meta = main(
        n, cap, page_counts, q, meta, cache_k, cache_v, pk, pv, decode_k[0], decode_v[0]
    )
    store_k, store_v = write(store_k, store_v)
    store_k, store_v, out, meta = lax.optimization_barrier((store_k, store_v, out, meta))
    out = out.reshape(KVH, 1 + STEPS, GROUP, HD).transpose(1, 0, 2, 3).reshape(1 + STEPS, HQ * HD)
    return (
        out[:1],
        out[1:].reshape(1, STEPS, HQ * HD),
        store_k.reshape(-1, KVD),
        store_v.reshape(-1, KVD),
        meta[:, :cap, ID_LANE].reshape(-1),
    )


def solution(mesh):
    both = ("groups", "seq")
    in_specs = (
        P(both, None),
        P(both, None),
        P(both, None),
        P("groups"),
        P(both, None),
        P(both, None, None),
        P(both, None, None),
        P(both, None, None),
        P(both),
    )
    out_specs = (
        P(both, None),
        P(both, None, None),
        P(both, None),
        P(both, None),
        P(both),
    )
    return jax.shard_map(
        per_device, mesh=mesh, in_specs=in_specs, out_specs=out_specs, check_vma=False
    )
```

profile of v0, /device:TPU:9, one launch (start us, length us, event | category | flops | bytes accessed | tf_op | source)
XLA Modules:
  0.0 121.6 jit_solution(16284235956888986547)
XLA Ops:
  0.6 0.0 copy-start.7
  0.6 0.0 copy-start.5
  0.7 0.0 copy-start.4
  1.3 0.8 reduce
  2.2 0.8 maximum_bitcast_fusion.q_ref
  3.0 0.0 copy-start
  3.0 1.2 copy-done
  4.2 0.0 copy-start.2
  4.2 1.2 %copy-done.2 = bf16[512,1024]{1,0:T(8,128)(2,1)S(1)} copy-done((bf16[512,1024]{1,0:T(8,128)(2,1)S(1)}, bf16[512,1024]{1,0:T(8,128)(2,1)}, u32[]{:S(2)}) %copy-start.2) | copy-done | bytes 1048600
  5.4 0.0 copy-start.6
  5.4 0.7 copy-done.6
  6.1 0.7 copy-done.8
  6.7 2.4 %pack.1 = (bf16[128,8,1024]{2,1,0:T(8,128)(2,1)S(1)}, bf16[128,8,1024]{2,1,0:T(8,128)(2,1)S(1)}, s32[16,8,128]{2,1,0:T(8,128)S(1)}) custom-call(s32[64]{0:T(128)S(1)} %bitcast.36, s32[16]{0:T(128)S(1)} %copy-done.6, s32[1]{0:T(128)S(6)} %copy.26.context, bf16[64,8,1024]{2,1,0:T(8,128)(2,1)S(1)} %bitcast.30, bf16[64,8,1024]{2,1,0:T(8,128)(2,1)S(1)} %bitcast.31), custom_call_target="tpu_custom_call" | custom-call | tf_op jit(solution)/shard_map/pack/pallas_call | solution.py:84
  9.1 0.0 copy-done.7
  9.2 0.0 copy-done.5
  9.2 0.0 copy-done.4
  9.2 0.0 copy-done.1
  9.2 0.0 copy-done.3
  9.2 108.1 %exchange.1 = (bf16[8,24,128]{2,1,0:T(8,128)(2,1)S(1)}, bf16[128,8,1024]{2,1,0:T(8,128)(2,1)S(1)}, bf16[128,8,1024]{2,1,0:T(8,128)(2,1)S(1)}, s32[16,8,128]{2,1,0:T(8,128)S(1)}) custom-call(s32[16]{0:T(128)S(1)} %copy-done.7, bf16[8,24,128]{2,1,0:T(8,128)(2,1)S(1)} %maximum_bitcast_fusion.q_ref, s32[16,8,128]{2,1,0:T(8,128)S(1)} %get-tuple-element.18.meta_ref, ...), custom_call_target="tpu_custom_call" | custom-call | tf_op jit(solution)/shard_map/exchange/pallas_call | solution.py:403
  117.3 2.0 %write.1 = (bf16[128,8,1024]{2,1,0:T(8,128)(2,1)}, bf16[128,8,1024]{2,1,0:T(8,128)(2,1)}) custom-call(bf16[128,8,1024]{2,1,0:T(8,128)(2,1)S(1)} %get-tuple-element.21.k_in, bf16[128,8,1024]{2,1,0:T(8,128)(2,1)S(1)} %get-tuple-element.22.v_in), custom_call_target="tpu_custom_call" | custom-call | tf_op jit(solution)/shard_map/write/pallas_call | solution.py:448
  119.3 0.4 slice_reduce_fusion
  119.7 0.6 reshape_squeeze.3
  120.3 0.6 reshape.43
  121.0 0.6 slice.14
  (6 shorter events, 0.0 us)
Async XLA Ops:
  0.6 8.5 %copy-start.7 = (s32[16]{0:T(128)S(1)}, s32[16]{0:T(128)}, u32[]{:S(2)}) copy-start(s32[16]{0:T(128)} %counts.3) | copy-start | bytes 196
  0.6 8.5 %copy-start.5 = (bf16[1,2,1024]{2,1,0:T(2,128)(2,1)S(1)}, bf16[1,2,1024]{2,1,0:T(2,128)(2,1)}, u32[]{:S(2)}) copy-start(bf16[1,2,1024]{2,1,0:T(2,128)(2,1)} %param.16) | copy-start | bytes 12292
  0.7 8.5 %copy-start.4 = (bf16[1,2,1024]{2,1,0:T(2,128)(2,1)S(1)}, bf16[1,2,1024]{2,1,0:T(2,128)(2,1)}, u32[]{:S(2)}) copy-start(bf16[1,2,1024]{2,1,0:T(2,128)(2,1)} %param.15) | copy-start | bytes 12292
  3.0 1.2 %copy-start = (bf16[512,1024]{1,0:T(8,128)(2,1)S(1)}, bf16[512,1024]{1,0:T(8,128)(2,1)}, u32[]{:S(2)}) copy-start(bf16[512,1024]{1,0:T(8,128)(2,1)} %ck_ref.1) | copy-start | bytes 3145732
  4.2 1.2 %copy-start.2 = (bf16[512,1024]{1,0:T(8,128)(2,1)S(1)}, bf16[512,1024]{1,0:T(8,128)(2,1)}, u32[]{:S(2)}) copy-start(bf16[512,1024]{1,0:T(8,128)(2,1)} %cv_ref.1) | copy-start | bytes 3145732
  5.4 0.7 copy-start.6
  6.1 0.7 copy-start.8
  6.7 2.5 %copy-start.1 = (bf16[512,1024]{1,0:T(8,128)(2,1)S(1)}, bf16[512,1024]{1,0:T(8,128)(2,1)}, u32[]{:S(2)}) copy-start(bf16[512,1024]{1,0:T(8,128)(2,1)} %ck_ref.1) | copy-start | bytes 3145732
  6.7 2.5 %copy-start.3 = (bf16[512,1024]{1,0:T(8,128)(2,1)S(1)}, bf16[512,1024]{1,0:T(8,128)(2,1)}, u32[]{:S(2)}) copy-start(bf16[512,1024]{1,0:T(8,128)(2,1)} %cv_ref.1) | copy-start | bytes 3145732
where the time goes:
time: 122 us
  Pallas kernels  112 us (92%)
  local copies, waits for them, and re-layouts  6.07 us (5%)
  other arithmetic  1.62 us (1%)
  between operations  1.41 us (1%)
    pallas_call x1, Pallas kernels, main(): pl.pallas_call(functools.partial(main_kernel, n, cap, chunk), in_specs=[s...  108 us
    unnamed x18, local copies, waits for them, and re-layouts  3.78 us

commit v1 on v0

--- a/solution.py
+++ b/solution.py
@@ -16,20 +16,41 @@
 GROUP = HQ // KVH
 ROWS = (1 + STEPS) * GROUP
 LANES = 128
-ID_LANE = 64
 MASKED = -1e30
 SCALE = HD ** (-0.5)
 MESH = pl.DeviceIdType.MESH
 
 META, KEYS, VALUES = range(3)
 QROW, PART, STAT = range(3)
-
-
-def pack_kernel(
-    n, cap, page_slots, owner, counts, context, ck_hbm, cv_hbm, out_k, out_v, meta,
-    ck, cv, table, seen, done,
+IDS, ROUTE = range(2)
+
+
+def plan(n, cap):
+    if n // 4 != 4 or n % 4:
+        return False, 0, 0
+    most = cap * n // 2
+    return True, most * 11 // 16, most // 2 * 7 // 8
+
+
+def pieces_of(parts):
+    width = KVD // parts
+    return [(kind, i * width, width) for kind in (KEYS, VALUES) for i in range(parts)]
+
+
+def prep_kernel(
+    n, cap, page_slots, split, dense, tail,
+    owner, counts, context, ck_hbm, cv_hbm, pq, dq,
+    out_k, out_v, *rest,
 ):
+    if split:
+        cross_k, cross_v, q_out, meta, ck, cv, table, seen, cross, tally, done = rest
+    else:
+        q_out, meta, ck, cv, table, seen, done = rest
     me = lax.axis_index("seq")
+    my_z, plane = me // 4, me % 4
+    half = my_z // 2
+    span = n // 2 if split else n
+    base = half * span if split else 0
     loads = [
         pltpu.make_async_copy(ck_hbm, ck, done.at[0]),
         pltpu.make_async_copy(cv_hbm, cv, done.at[1]),
@@ -37,81 +58,171 @@
     for load in loads:
         load.start()
 
+    for s in range(1 + STEPS):
+        for h in range(HQ):
+            row = s * GROUP + h % GROUP
+            src = pq if s == 0 else dq
+            at = 0 if s == 0 else s - 1
+            q_out[h // GROUP, row : row + 1, :] = src[at : at + 1, h * HD : (h + 1) * HD]
+
     def clear(i, _):
         seen[i] = 0
         for k in range(cap):
             table[i * cap + k] = -1
+            meta[i, IDS, me * cap + k] = -1
+        meta[i, ROUTE, 4 * cap] = context[0]
         return 0
 
     lax.fori_loop(0, n, clear, 0)
+    if split:
+        near = (2 - half) * 4 + plane
+        far = 3 * (1 - half) * 4 + plane
+        for k in range(4 * cap):
+            meta[near, ROUTE, k] = -1
+            meta[far, ROUTE, k] = -1
+
+        def zero(i, _):
+            cross[i] = 0
+            return 0
+
+        lax.fori_loop(0, dense, zero, 0)
+        tally[0] = 0
+        tally[1] = 0
+        tally[2] = 0
 
     def place(j, _):
         o = owner[j]
         k = seen[o]
         seen[o] = k + 1
         table[o * cap + k] = j
+        meta[o, IDS, me * cap + k] = me * page_slots + j
+        if split:
+            @pl.when(o // 4 // 2 != half)
+            def _():
+                front, back = tally[0], tally[1]
+                room = front + back < dense
+                at = (o % 4) * cap + k
+
+                @pl.when(room & (o // 4 == 2 - half))
+                def _():
+                    cross[front] = j
+                    meta[near, ROUTE, at] = front
+                    tally[0] = front + 1
+
+                fits = room & (back < tail)
+
+                @pl.when(fits & (o // 4 != 2 - half))
+                def _():
+                    cross[dense - 1 - back] = j
+                    meta[far, ROUTE, at] = tail - 1 - back
+                    tally[1] = back + 1
+
+                @pl.when(jnp.logical_not(jnp.where(o // 4 == 2 - half, room, fits)))
+                def _():
+                    tally[2] = 1
+
         return 0
 
     lax.fori_loop(0, counts[me], place, 0)
+
+    if split:
+        def flag(i, _):
+            meta[i, ROUTE, 4 * cap + 1] = tally[2]
+            return 0
+
+        lax.fori_loop(0, n, flag, 0)
 
     for load in loads:
         load.wait()
 
-    tile_row = lax.broadcasted_iota(jnp.int32, (8, LANES), 0)
-    lane = lax.broadcasted_iota(jnp.int32, (8, LANES), 1)
-
-    def fill(dst, _):
-        ids = jnp.full((8, LANES), -1, jnp.int32)
+    if split:
+        def pick(i, _):
+            page = cross[i]
+            cross_k[i] = ck[page]
+            cross_v[i] = cv[page]
+            return 0
+
+        lax.fori_loop(0, dense, pick, 0)
+
+    def fill(i, _):
         for k in range(cap):
-            slot = dst * cap + k
-            src = table[slot]
+            src = table[(base + i) * cap + k]
             page = jnp.maximum(src, 0)
             there = jnp.full((PAGE, KVD), src, jnp.int32) >= 0
-            out_k[slot] = jnp.where(there, ck[page], jnp.zeros((), out_k.dtype))
-            out_v[slot] = jnp.where(there, cv[page], jnp.zeros((), out_v.dtype))
-            ids = jnp.where(tile_row == k, jnp.where(src >= 0, me * page_slots + src, -1), ids)
-        meta[dst] = jnp.where(lane < ID_LANE, context[0], ids)
+            out_k[i * cap + k] = jnp.where(there, ck[page], jnp.zeros((), out_k.dtype))
+            out_v[i * cap + k] = jnp.where(there, cv[page], jnp.zeros((), out_v.dtype))
         return 0
 
-    lax.fori_loop(0, n, fill, 0)
-
-
-def pack(n, cap, owner, counts, context, ck, cv):
+    lax.fori_loop(0, span, fill, 0)
+
+
+def prep(n, cap, split, owner, counts, context, ck, cv, pq, dq):
     page_slots = ck.shape[0]
+    _, dense, tail = plan(n, cap)
     smem = pl.BlockSpec(memory_space=pltpu.SMEM)
     vmem = pl.BlockSpec(memory_space=pltpu.VMEM)
-    hbm = pl.BlockSpec(memory_space=pl.ANY)
+    hbm = pl.BlockSpec(memory_space=pltpu.HBM)
+    span = n // 2 if split else n
+
+    def pages(count):
+        return [jax.ShapeDtypeStruct((count, PAGE, KVD), x.dtype) for x in (ck, cv)]
+
+    out_shape = pages(span * cap) + (pages(dense) if split else [])
+    out_specs = [vmem] * len(out_shape) + [vmem, smem]
+    out_shape += [
+        jax.ShapeDtypeStruct((KVH, ROWS, HD), pq.dtype),
+        jax.ShapeDtypeStruct((n, 2, n * cap), jnp.int32),
+    ]
+    scratch = [
+        pltpu.VMEM(ck.shape, ck.dtype), pltpu.VMEM(cv.shape, cv.dtype),
+        pltpu.SMEM((n * cap,), jnp.int32), pltpu.SMEM((n,), jnp.int32),
+    ]
+    if split:
+        scratch += [pltpu.SMEM((dense,), jnp.int32), pltpu.SMEM((4,), jnp.int32)]
     return pl.pallas_call(
-        functools.partial(pack_kernel, n, cap, page_slots),
-        in_specs=[smem, smem, smem, hbm, hbm],
-        out_specs=(vmem, vmem, vmem),
-        out_shape=(
-            jax.ShapeDtypeStruct((n * cap, PAGE, KVD), ck.dtype),
-            jax.ShapeDtypeStruct((n * cap, PAGE, KVD), cv.dtype),
-            jax.ShapeDtypeStruct((n, 8, LANES), jnp.int32),
-        ),
-        scratch_shapes=[
-            pltpu.VMEM(ck.shape, ck.dtype), pltpu.VMEM(cv.shape, cv.dtype),
-            pltpu.SMEM((n * cap,), jnp.int32), pltpu.SMEM((n,), jnp.int32),
-            pltpu.SemaphoreType.DMA((2,)),
-        ],
+        functools.partial(prep_kernel, n, cap, page_slots, split, dense, tail),
+        in_specs=[smem, smem, smem, hbm, hbm, vmem, vmem],
+        out_specs=out_specs,
+        out_shape=out_shape,
+        scratch_shapes=scratch + [pltpu.SemaphoreType.DMA((2,))],
         compiler_params=pltpu.CompilerParams(vmem_limit_bytes=16 << 20),
-        name="pack",
-    )(owner, counts, context, ck, cv)
+        name="prep",
+    )(owner, counts, context, ck, cv, pq, dq)
 
 
 def main_kernel(
-    n, cap, chunk, counts, q_ref, meta_ref, ck_ref, cv_ref, pk_ref, pv_ref, ok_ref, ov_ref,
-    out_ref, store_k, store_v, meta_out,
-    qbuf, obuf, stat, limit, got1, got1s, obuf1, stat1, got2, got2s, obuf2, stat2, pbuf, sbuf,
-    page_send, page_recv, row_send, row_recv, pair_send, pair_recv, local,
+    n, cap, chunk, split, dense, tail, parts,
+    counts, q_ref, meta_ref, ck_hbm, cv_hbm, pk_ref, pv_ref, ok_ref, ov_ref, *rest,
 ):
+    if split:
+        mk_ref, mv_ref = rest[:2]
+        rest = rest[2:]
+    pre_out, dec_out, store_k, store_v, meta_out = rest[:5]
+    rest = rest[5:]
+    if split:
+        flag_out = rest[0]
+        rest = rest[1:]
+    (
+        ck_ref, cv_ref, meta_s,
+        qbuf, obuf, stat, limit, got1, got1s, obuf1, stat1, got2, got2s, obuf2, stat2, pbuf, sbuf,
+        page_send, page_recv, row_send, row_recv, pair_send, pair_recv, local,
+    ) = rest[:24]
+    rest = rest[24:]
+    if split:
+        (
+            meta_x, meta_xs, *lands, fan_k, fan_v,
+            x_send, x_recv, cross_send, cross_recv, pass_send, pass_recv, fan_send, fan_recv,
+        ) = rest
     depth = n // 4
+    groups = lax.axis_size("groups")
+    my_g = lax.axis_index("groups")
     me = lax.axis_index("seq")
     my_z, my_y, my_c = me // 4, (me // 2) % 2, me % 2
-    block = (my_c * 2 + my_y) * depth + my_z
+    plane = me % 4
+    half = my_z // 2
     across = my_z * 4 + (1 - my_y) * 2 + my_c
     sibling = my_z * 4 + my_y * 2 + (1 - my_c)
+    base = half * (n // 2) if split else 0
 
     def rows_of(first, count=1):
         return pl.ds(pl.multiple_of(first * ROWS, 8), count * ROWS)
@@ -123,11 +234,11 @@
         if kind == META:
             return meta_ref.at[peer], meta_out.at[writer]
         if kind == KEYS:
-            return pk_ref.at[slots_of(peer)], store_k.at[slots_of(writer)]
-        return pv_ref.at[slots_of(peer)], store_v.at[slots_of(writer)]
+            return pk_ref.at[slots_of(peer - base)], store_k.at[slots_of(writer)]
+        return pv_ref.at[slots_of(peer - base)], store_v.at[slots_of(writer)]
 
     def page(kind, peer, arriving=False):
-        src, dst = page_ends(kind, peer, peer if arriving else me)
+        src, dst = page_ends(kind, me if arriving else peer, peer if arriving else me)
         return pltpu.make_async_remote_copy(
             src_ref=src, dst_ref=dst, send_sem=page_send.at[kind, peer],
             recv_sem=page_recv.at[kind, peer if arriving else me],
@@ -170,13 +281,108 @@
 
         lax.fori_loop(1, count, step, 0)
 
+    caches = [
+        pltpu.make_async_copy(ck_hbm, ck_ref, local.at[6]),
+        pltpu.make_async_copy(cv_hbm, cv_ref, local.at[7]),
+    ]
+    for load in caches:
+        load.start()
+
     barrier = pltpu.get_barrier_semaphore()
 
     def greet(peer):
         pl.semaphore_signal(barrier, inc=1, device_id={"seq": peer}, device_id_type=MESH)
 
+    def greet_group(g):
+        pl.semaphore_signal(barrier, inc=1, device_id={"groups": g}, device_id_type=MESH)
+
     each(n, me, greet)
-    pl.semaphore_wait(barrier, n - 1)
+    if split:
+        each(groups, my_g, greet_group)
+    pl.semaphore_wait(barrier, n - 1 + (groups - 1 if split else 0))
+
+    if split:
+        pieces = pieces_of(parts)
+        mine_near = my_z == 1 + half
+        other = (1 - half) * 2
+        HEAD, TAIL = 0, 1
+        spans = (pl.ds(0, dense - tail), pl.ds(dense - tail, tail))
+
+        def cross(piece, end, zi):
+            kind, col, width = pieces[piece]
+            src = mk_ref if kind == KEYS else mv_ref
+            return pltpu.make_async_remote_copy(
+                src_ref=src.at[spans[end], :, pl.ds(col, width)],
+                dst_ref=lands[piece].at[zi, spans[end]],
+                send_sem=cross_send.at[piece, end], recv_sem=cross_recv.at[piece, end, zi],
+                device_id={"seq": (2 - half) * 4 + plane}, device_id_type=MESH,
+            )
+
+        def hand(piece, zi):
+            buf = lands[piece]
+            return pltpu.make_async_remote_copy(
+                src_ref=buf.at[zi, spans[TAIL]], dst_ref=buf.at[zi, pl.ds(0, tail)],
+                send_sem=pass_send.at[piece, zi], recv_sem=pass_recv.at[piece, zi],
+                device_id={"seq": 3 * half * 4 + plane}, device_id_type=MESH,
+            )
+
+        def fan(piece, zi, to, writer):
+            kind, col, width = pieces[piece]
+            src = fan_k if kind == KEYS else fan_v
+            dst = store_k if kind == KEYS else store_v
+            cols = pl.ds(col, width)
+            shard = (other + zi) * 4 + writer
+            return pltpu.make_async_remote_copy(
+                src_ref=src.at[zi, to, :, :, cols], dst_ref=dst.at[slots_of(shard), :, cols],
+                send_sem=fan_send.at[piece, zi, to], recv_sem=fan_recv.at[piece, zi, writer],
+                device_id={"seq": my_z * 4 + to}, device_id_type=MESH,
+            )
+
+        def launch(piece, end):
+            cross(piece, end, my_z % 2).start()
+
+        def pass_on(piece):
+            @pl.when(mine_near)
+            def _():
+                for zi in range(2):
+                    cross(piece, TAIL, zi).wait_recv()
+                    hand(piece, zi).start()
+
+        def unpack(piece):
+            kind, col, width = pieces[piece]
+            buf = lands[piece]
+            out = fan_k if kind == KEYS else fan_v
+            keep = store_k if kind == KEYS else store_v
+            cols = pl.ds(col, width)
+
+            @pl.when(mine_near)
+            def _():
+                for zi in range(2):
+                    cross(piece, HEAD, zi).wait_recv()
+
+            @pl.when(jnp.logical_not(mine_near))
+            def _():
+                for zi in range(2):
+                    hand(piece, zi).wait_recv()
+
+            for zi in range(2):
+                shard = (other + zi) * 4 + plane
+
+                def page_at(to, k):
+                    at = meta_s[shard, ROUTE, to * cap + k]
+                    there = jnp.full((PAGE, width), at, jnp.int32) >= 0
+                    return jnp.where(
+                        there, buf[zi, jnp.maximum(at, 0)], jnp.zeros((), buf.dtype)
+                    )
+
+                def send(to):
+                    for k in range(cap):
+                        out[zi, to, k, :, cols] = page_at(to, k)
+                    fan(piece, zi, to, plane).start()
+
+                each(4, plane, send)
+                for k in range(cap):
+                    keep[shard * cap + k, :, cols] = page_at(plane, k)
 
     each(depth, my_z, lambda z: row(QROW, z).start())
     own_row(QROW).start()
@@ -188,17 +394,28 @@
         page(KEYS, peer).start()
         page(VALUES, peer).start()
 
-    def near(i, _):
-        z = lax.rem(my_z + depth // 2 + i, depth)
-
-        @pl.when(z != my_z)
-        def _():
-            start_pages(z * 4 + my_y * 2 + my_c)
-            start_pages(z * 4 + my_y * 2 + (1 - my_c))
-
-        return 0
-
-    lax.fori_loop(0, depth, near, 0)
+    if split:
+        first = half * 2
+        other_z = first + (1 - my_z % 2)
+        order = [(p, TAIL) for p in range(len(pieces))] + [(p, HEAD) for p in range(len(pieces))]
+        late = [(p, HEAD) for p in range(parts, 2 * parts)]
+        for item in order:
+            if item not in late:
+                launch(*item)
+        start_pages(other_z * 4 + plane)
+        start_pages(other_z * 4 + my_y * 2 + (1 - my_c))
+    else:
+        def near(i, _):
+            z = lax.rem(my_z + depth // 2 + i, depth)
+
+            @pl.when(z != my_z)
+            def _():
+                start_pages(z * 4 + my_y * 2 + my_c)
+                start_pages(z * 4 + my_y * 2 + (1 - my_c))
+
+            return 0
+
+        lax.fori_loop(0, depth, near, 0)
 
     own_row(QROW).wait()
     each(depth, my_z, lambda z: row(QROW, z, True).wait_recv())
@@ -211,6 +428,18 @@
     pair(1, q_c_out, q_c_out, sibling).start()
     own_page(META).wait()
     each(n, me, lambda peer: page(META, peer, True).wait_recv())
+    table = pltpu.make_async_copy(meta_out, meta_s, local.at[8])
+    table.start()
+    if split:
+        def share(g, arriving=False):
+            return pltpu.make_async_remote_copy(
+                src_ref=meta_out, dst_ref=meta_x.at[g if arriving else my_g],
+                send_sem=x_send.at[g], recv_sem=x_recv.at[g if arriving else my_g],
+                device_id={"groups": g}, device_id_type=MESH,
+            )
+
+        each(groups, my_g, lambda g: share(g).start())
+    table.wait()
 
     live = PAGE * counts[me]
     start = PAGE * lax.fori_loop(
@@ -220,18 +449,19 @@
 
     def set_limit(p, _):
         d = (p % depth) * 4 + ((p // depth) % 2) * 2 + p // (2 * depth)
-        base = pl.multiple_of(p * ROWS, 8)
-        context = jnp.broadcast_to(meta_out[d][:, 0:1], (8, LANES))
-        reach = jnp.minimum(live, context - start)
-        limit[pl.ds(base, 8), :] = jnp.full(
+        at = pl.multiple_of(p * ROWS, 8)
+        reach = jnp.minimum(live, meta_s[d, ROUTE, 4 * cap] - start)
+        limit[pl.ds(at, 8), :] = jnp.full(
             (8, LANES), jnp.minimum(live, prompt - n + d + 1 - start)
         )
         for s in range(STEPS):
-            limit[pl.ds(pl.multiple_of(base + 8 * (s + 1), 8), 8), :] = reach
+            limit[pl.ds(pl.multiple_of(at + 8 * (s + 1), 8), 8), :] = jnp.full((8, LANES), reach)
         return 0
 
     lax.fori_loop(0, n, set_limit, 0)
     pair(1, q_c_out, q_c_in, sibling).wait_recv()
+    for load in caches:
+        load.wait()
 
     def far(i, _):
         z = lax.rem(my_z + depth // 2 + i, depth)
@@ -239,7 +469,11 @@
         start_pages(z * 4 + (1 - my_y) * 2 + (1 - my_c))
         return 0
 
-    far(0, 0)
+    if split:
+        start_pages(other_z * 4 + (1 - my_y) * 2 + my_c)
+        start_pages(other_z * 4 + (1 - my_y) * 2 + (1 - my_c))
+    else:
+        far(0, 0)
 
     lane = lax.broadcasted_iota(jnp.int32, (chunk, LANES), 1)
     keys = ck_ref.shape[0]
@@ -297,6 +531,9 @@
     part1s = pair(3, stat.at[rows_of(give, 2 * depth), :], got1s, sibling)
     part1s.start()
     part1.start()
+    if split:
+        for piece in range(parts):
+            pass_on(piece)
     part1s.wait_recv()
     part1.wait_recv()
     merge(obuf, stat, my_c * 2 * depth, got1, got1s, obuf1, stat1)
@@ -330,7 +567,17 @@
     own_row(STAT).start()
     own_row(PART).start()
 
-    lax.fori_loop(1, depth, far, 0)
+    if split:
+        for item in late:
+            launch(*item)
+        start_pages(my_z * 4 + (1 - my_y) * 2 + my_c)
+        start_pages(my_z * 4 + (1 - my_y) * 2 + (1 - my_c))
+        for piece in range(parts, 2 * parts):
+            pass_on(piece)
+        for piece in range(parts):
+            unpack(piece)
+    else:
+        lax.fori_loop(1, depth, far, 0)
 
     own_row(STAT).wait()
     own_row(PART).wait()
@@ -363,7 +610,34 @@
 
     norm, sums = lax.fori_loop(0, depth, add, (norm, tuple(sums)))
     for g in range(KVH):
-        out_ref[g] = (sums[g] / norm[:, g : g + 1]).astype(out_ref.dtype)
+        result = (sums[g] / norm[:, g : g + 1]).astype(pre_out.dtype)
+        for h in range(GROUP):
+            at = (g * GROUP + h) * HD
+            pre_out[0:1, at : at + HD] = result[h : h + 1]
+            for s in range(STEPS):
+                r = (s + 1) * GROUP + h
+                dec_out[s : s + 1, at : at + HD] = result[r : r + 1]
+
+    if split:
+        for piece in range(parts, 2 * parts):
+            unpack(piece)
+        each(groups, my_g, lambda g: share(g, True).wait_recv())
+        tables = pltpu.make_async_copy(meta_x, meta_xs, local.at[9])
+        tables.start()
+        tables.wait()
+
+        def worst(i, sofar):
+            return jnp.maximum(sofar, meta_s[i, ROUTE, 4 * cap + 1])
+
+        over = lax.fori_loop(0, n, worst, jnp.int32(0))
+        for other_g in range(groups):
+            def worse(i, sofar):
+                return jnp.maximum(
+                    sofar, jnp.where(my_g == other_g, 0, meta_xs[other_g, i, ROUTE, 4 * cap + 1])
+                )
+
+            over = lax.fori_loop(0, n, worse, over)
+        flag_out[0] = over
 
     pair(0, q_y_out, q_y_out, across).wait_send()
     pair(1, q_c_out, q_c_out, sibling).wait_send()
@@ -377,21 +651,43 @@
     each(depth, my_z, finish_row)
     own_page(KEYS).wait()
     own_page(VALUES).wait()
+    each(n, me, lambda peer: page(META, peer).wait_send())
 
     def finish(peer):
         page(KEYS, peer, True).wait_recv()
         page(VALUES, peer, True).wait_recv()
-        for kind in (META, KEYS, VALUES):
+        for kind in (KEYS, VALUES):
             page(kind, peer).wait_send()
 
-    each(n, me, finish)
-
-
-def main(n, cap, counts, q, meta, ck, cv, pk, pv, own_k, own_v):
+    if split:
+        each(groups, my_g, lambda g: share(g).wait_send())
+        each(n // 2, me - base, lambda i: finish(base + i))
+        for item in order:
+            cross(*item, my_z % 2).wait_send()
+        for piece in range(2 * parts):
+            @pl.when(mine_near)
+            def _():
+                for zi in range(2):
+                    hand(piece, zi).wait_send()
+
+            for zi in range(2):
+                def settle(to):
+                    fan(piece, zi, to, plane).wait_send()
+                    fan(piece, zi, to, to).wait_recv()
+
+                each(4, plane, settle)
+    else:
+        each(n, me, finish)
+
+
+def main(n, cap, split, groups, counts, q, meta, ck, cv, pk, pv, own_k, own_v, cross):
     height = n * ROWS
     chunk = min(height, 384)
+    _, dense, tail = plan(n, cap)
+    parts_count = 2
     vmem = pl.BlockSpec(memory_space=pltpu.VMEM)
     smem = pl.BlockSpec(memory_space=pltpu.SMEM)
+    hbm = pl.BlockSpec(memory_space=pltpu.HBM)
 
     def parts(rows):
         return pltpu.VMEM((KVH, rows, HD), jnp.bfloat16)
@@ -400,89 +696,201 @@
         return pltpu.VMEM((rows, LANES), jnp.float32)
 
     half, quarter, depth = height // 2, height // 4, n // 4
+    store = (n * cap, PAGE, KVD)
+    out_shape = [
+        jax.ShapeDtypeStruct((1, HQ * HD), q.dtype),
+        jax.ShapeDtypeStruct((STEPS, HQ * HD), q.dtype),
+        jax.ShapeDtypeStruct(store, pk.dtype),
+        jax.ShapeDtypeStruct(store, pv.dtype),
+        jax.ShapeDtypeStruct(meta.shape, meta.dtype),
+    ]
+    out_specs = [vmem] * 5
+    scratch = [
+        pltpu.VMEM(ck.shape, ck.dtype), pltpu.VMEM(cv.shape, cv.dtype),
+        pltpu.SMEM(meta.shape, jnp.int32),
+        parts(height), parts(height), stats(height), pltpu.VMEM((height, LANES), jnp.int32),
+        parts(half), stats(half), parts(half), stats(half),
+        parts(quarter), stats(quarter), parts(quarter), stats(quarter),
+        pltpu.VMEM((depth, KVH, ROWS, HD), jnp.bfloat16),
+        pltpu.VMEM((depth, ROWS, LANES), jnp.float32),
+        pltpu.SemaphoreType.DMA((3, n)),
+        pltpu.SemaphoreType.DMA((3, n)),
+        pltpu.SemaphoreType.DMA((3, depth)),
+        pltpu.SemaphoreType.DMA((3, depth)),
+        pltpu.SemaphoreType.DMA((6,)),
+        pltpu.SemaphoreType.DMA((6,)),
+        pltpu.SemaphoreType.DMA((10,)),
+    ]
+    if split:
+        out_shape.append(jax.ShapeDtypeStruct((1,), jnp.int32))
+        out_specs.append(smem)
+        count = 2 * parts_count
+        scratch += [
+            pltpu.VMEM((groups,) + meta.shape, jnp.int32),
+            pltpu.SMEM((groups,) + meta.shape, jnp.int32),
+            *[pltpu.VMEM((2, dense, PAGE, w), pk.dtype) for _, _, w in pieces_of(parts_count)],
+            pltpu.VMEM((2, 4, cap, PAGE, KVD), pk.dtype),
+            pltpu.VMEM((2, 4, cap, PAGE, KVD), pv.dtype),
+            pltpu.SemaphoreType.DMA((groups,)),
+            pltpu.SemaphoreType.DMA((groups,)),
+            pltpu.SemaphoreType.DMA((count, 2)),
+            pltpu.SemaphoreType.DMA((count, 2, 2)),
+            pltpu.SemaphoreType.DMA((count, 2)),
+            pltpu.SemaphoreType.DMA((count, 2)),
+            pltpu.SemaphoreType.DMA((count, 2, 4)),
+            pltpu.SemaphoreType.DMA((count, 2, 4)),
+        ]
     return pl.pallas_call(
-        functools.partial(main_kernel, n, cap, chunk),
-        in_specs=[smem] + [vmem] * 8,
-        out_specs=(vmem, vmem, vmem, vmem),
-        out_shape=(
-            jax.ShapeDtypeStruct((KVH, ROWS, HD), jnp.bfloat16),
-            jax.ShapeDtypeStruct(pk.shape, pk.dtype),
-            jax.ShapeDtypeStruct(pv.shape, pv.dtype),
-            jax.ShapeDtypeStruct(meta.shape, meta.dtype),
-        ),
-        scratch_shapes=[
-            parts(height), parts(height), stats(height), pltpu.VMEM((height, LANES), jnp.int32),
-            parts(half), stats(half), parts(half), stats(half),
-            parts(quarter), stats(quarter), parts(quarter), stats(quarter),
-            pltpu.VMEM((depth, KVH, ROWS, HD), jnp.bfloat16),
-            pltpu.VMEM((depth, ROWS, LANES), jnp.float32),
-            pltpu.SemaphoreType.DMA((3, n)),
-            pltpu.SemaphoreType.DMA((3, n)),
-            pltpu.SemaphoreType.DMA((3, depth)),
-            pltpu.SemaphoreType.DMA((3, depth)),
-            pltpu.SemaphoreType.DMA((6,)),
-            pltpu.SemaphoreType.DMA((6,)),
-            pltpu.SemaphoreType.DMA((6,)),
-        ],
+        functools.partial(main_kernel, n, cap, chunk, split, dense, tail, parts_count),
+        in_specs=[smem] + [vmem] * 2 + [hbm] * 2 + [vmem] * (4 + len(cross)),
+        out_specs=out_specs,
+        out_shape=out_shape,
+        scratch_shapes=scratch,
         compiler_params=pltpu.CompilerParams(
             collective_id=0, has_side_effects=True, vmem_limit_bytes=32 << 20
         ),
         name="exchange",
-    )(counts, q, meta, ck, cv, pk, pv, own_k, own_v)
-
-
-def write_kernel(k_in, v_in, k_out, v_out, done):
+    )(counts, q, meta, ck, cv, pk, pv, own_k, own_v, *cross)
+
+
+def direct_kernel(n, cap, pk_ref, pv_ref, store_k, store_v, send, recv, local):
+    me = lax.axis_index("seq")
+
+    def slots_of(d):
+        return pl.ds(d * cap, cap)
+
+    def ends(kind, to, writer):
+        src, dst = (pk_ref, store_k) if kind == 0 else (pv_ref, store_v)
+        return src.at[slots_of(to)], dst.at[slots_of(writer)]
+
+    def page(kind, peer, arriving=False):
+        src, dst = ends(kind, peer, peer if arriving else me)
+        return pltpu.make_async_remote_copy(
+            src_ref=src, dst_ref=dst, send_sem=send.at[kind, peer],
+            recv_sem=recv.at[kind, peer if arriving else me],
+            device_id={"seq": peer}, device_id_type=MESH,
+        )
+
+    def each(body):
+        def step(i, _):
+            body(lax.rem(me + i, n))
+            return 0
+
+        lax.fori_loop(1, n, step, 0)
+
+    barrier = pltpu.get_barrier_semaphore()
+    each(
+        lambda peer: pl.semaphore_signal(
+            barrier, inc=1, device_id={"seq": peer}, device_id_type=MESH
+        )
+    )
+    pl.semaphore_wait(barrier, n - 1)
+    own = []
+    for kind in range(2):
+        each(lambda peer: page(kind, peer).start())
+        src, dst = ends(kind, me, me)
+        own.append(pltpu.make_async_copy(src, dst, local.at[kind]))
+        own[-1].start()
+    for kind in range(2):
+        own[kind].wait()
+        each(lambda peer: page(kind, peer, True).wait_recv())
+        each(lambda peer: page(kind, peer).wait_send())
+
+
+def direct(n, cap, pk, pv):
+    vmem = pl.BlockSpec(memory_space=pltpu.VMEM)
+    return pl.pallas_call(
+        functools.partial(direct_kernel, n, cap),
+        in_specs=[vmem] * 2,
+        out_specs=[vmem] * 2,
+        out_shape=[jax.ShapeDtypeStruct(x.shape, x.dtype) for x in (pk, pv)],
+        scratch_shapes=[
+            pltpu.SemaphoreType.DMA((2, n)),
+            pltpu.SemaphoreType.DMA((2, n)),
+            pltpu.SemaphoreType.DMA((2,)),
+        ],
+        compiler_params=pltpu.CompilerParams(
+            collective_id=1, has_side_effects=True, vmem_limit_bytes=16 << 20
+        ),
+        name="direct",
+    )(pk, pv)
+
+
+def write_kernel(
+    n, cap, k_in, v_in, pre_in, dec_in, meta_in,
+    k_out, v_out, pre_out, dec_out, ids_out, ids, done,
+):
     copies = [
         pltpu.make_async_copy(k_in, k_out, done.at[0]),
         pltpu.make_async_copy(v_in, v_out, done.at[1]),
+        pltpu.make_async_copy(pre_in, pre_out, done.at[2]),
+        pltpu.make_async_copy(dec_in, dec_out, done.at[3]),
     ]
     for copy in copies:
         copy.start()
-    for copy in copies:
+    lane = lax.broadcasted_iota(jnp.int32, (1, n * cap), 1)
+    row = meta_in[0, IDS : IDS + 1, :]
+    for s in range(1, n):
+        row = jnp.where(lane // cap == s, meta_in[s, IDS : IDS + 1, :], row)
+    ids[...] = row
+    last = pltpu.make_async_copy(ids, ids_out, done.at[4])
+    last.start()
+    for copy in copies + [last]:
         copy.wait()
 
 
-def write(store_k, store_v):
+def write(n, cap, store_k, store_v, pre, dec, meta):
     vmem = pl.BlockSpec(memory_space=pltpu.VMEM)
-    hbm = pl.BlockSpec(memory_space=pl.ANY)
+    hbm = pl.BlockSpec(memory_space=pltpu.HBM)
     return pl.pallas_call(
-        write_kernel,
-        in_specs=[vmem, vmem],
-        out_specs=(hbm, hbm),
-        out_shape=(
-            jax.ShapeDtypeStruct(store_k.shape, store_k.dtype),
-            jax.ShapeDtypeStruct(store_v.shape, store_v.dtype),
-        ),
-        scratch_shapes=[pltpu.SemaphoreType.DMA((2,))],
+        functools.partial(write_kernel, n, cap),
+        in_specs=[vmem] * 5,
+        out_specs=[hbm] * 5,
+        out_shape=[jax.ShapeDtypeStruct(x.shape, x.dtype) for x in (store_k, store_v, pre, dec)]
+        + [jax.ShapeDtypeStruct((1, n * cap), jnp.int32)],
+        scratch_shapes=[pltpu.VMEM((1, n * cap), jnp.int32), pltpu.SemaphoreType.DMA((5,))],
         compiler_params=pltpu.CompilerParams(vmem_limit_bytes=16 << 20),
         name="write",
-    )(store_k, store_v)
+    )(store_k, store_v, pre, dec, meta)
 
 
 def per_device(
     prefill_q, cache_k, cache_v, page_counts, page_owner, decode_q, decode_k, decode_v, context_len
 ):
     n = lax.axis_size("seq")
-    me = lax.axis_index("seq")
+    groups = lax.axis_size("groups")
     page_slots = cache_k.shape[0] // PAGE
     cap = max(2, 2 * page_slots // n)
+    split, _, _ = plan(n, cap)
     ck = cache_k.reshape(page_slots, PAGE, KVD)
     cv = cache_v.reshape(page_slots, PAGE, KVD)
-    pk, pv, meta = pack(n, cap, page_owner[:, 0], page_counts, context_len, ck, cv)
-    q = jnp.concatenate((prefill_q, decode_q[0]), axis=0)
-    q = q.reshape(1 + STEPS, KVH, GROUP, HD).transpose(1, 0, 2, 3).reshape(KVH, ROWS, HD)
-    out, store_k, store_v, meta = main(
-        n, cap, page_counts, q, meta, cache_k, cache_v, pk, pv, decode_k[0], decode_v[0]
+    owner = page_owner[:, 0]
+    parts = (page_counts, context_len, ck, cv, prefill_q, decode_q[0])
+    pk, pv, *cross, q, meta = prep(n, cap, split, owner, *parts)
+    pre, dec, store_k, store_v, meta, *flag = main(
+        n, cap, split, groups, page_counts, q, meta, cache_k, cache_v, pk, pv,
+        decode_k[0], decode_v[0], cross,
     )
-    store_k, store_v = write(store_k, store_v)
-    store_k, store_v, out, meta = lax.optimization_barrier((store_k, store_v, out, meta))
-    out = out.reshape(KVH, 1 + STEPS, GROUP, HD).transpose(1, 0, 2, 3).reshape(1 + STEPS, HQ * HD)
+
+    def keep(sk, sv, pre, dec, meta):
+        return write(n, cap, sk, sv, pre, dec, meta)
+
+    def again(sk, sv, pre, dec, meta):
+        pk, pv, _, _ = prep(n, cap, False, owner, *parts)
+        sk, sv = direct(n, cap, pk, pv)
+        return write(n, cap, sk, sv, pre, dec, meta)
+
+    if split:
+        results = lax.cond(flag[0][0] > 0, again, keep, store_k, store_v, pre, dec, meta)
+    else:
+        results = keep(store_k, store_v, pre, dec, meta)
+    store_k, store_v, pre, dec, ids = results
     return (
-        out[:1],
-        out[1:].reshape(1, STEPS, HQ * HD),
+        pre,
+        dec.reshape(1, STEPS, HQ * HD),
         store_k.reshape(-1, KVD),
         store_v.reshape(-1, KVD),
-        meta[:, :cap, ID_LANE].reshape(-1),
+        ids.reshape(-1),
     )
 
 

time: 122 us -> 120 us (0.984)
  the two profiles are of different devices: /device:TPU:9 before, /device:TPU:1 now
where the time goes in v1:
time: 120 us; the launch traced here: 119 us
  Pallas kernels  117 us (98%)
  between operations  2.19 us (2%)
    pallas_call x1, Pallas kernels, main(): pl.pallas_call(functools.partial(main_kernel, n, cap, chunk, split, dense...  111 us
    pallas_call x1, Pallas kernels, prep(): pl.pallas_call(functools.partial(prep_kernel, n, cap, page_slots, split,...  4.43 us

profile of v1, /device:TPU:1, one launch (start us, length us, event | category | flops | bytes accessed | tf_op | source)
XLA Modules:
  0.0 119.4 jit_solution(12164290977630564581)
XLA Ops:
  0.6 0.0 copy-start.6
  0.6 0.0 copy-start.3
  0.7 0.0 copy-start.2
  0.7 0.0 copy-start.1
  0.7 0.0 copy-start
  1.5 4.4 %prep.4 = (bf16[64,8,1024]{2,1,0:T(8,128)(2,1)S(1)}, bf16[64,8,1024]{2,1,0:T(8,128)(2,1)S(1)}, bf16[44,8,1024]{2,1,0:T(8,128)(2,1)S(1)}, bf16[44,8,1024]{2,1,0:T...) custom-call(s32[64]{0:T(128)} %bitcast.23, s32[16]{0:T(128)} %counts.3, s32[1]{0:T(128)S(6)} %copy.24.context, ...), custom_call_target="tpu_custom_call" | custom-call | tf_op jit(solution)/shard_map/prep/pallas_call | solution.py:182
  5.9 0.0 copy-done.6
  5.9 0.0 copy-done.3
  5.9 0.0 copy-done.2
  5.9 0.0 copy-done.1
  6.0 0.0 copy-done
  6.0 0.0 copy-start.4
  6.0 0.0 copy-start.5
  6.0 0.0 copy-start.7
  6.0 110.7 %exchange.1 = (bf16[1,8192]{1,0:T(2,128)(2,1)S(1)}, bf16[2,8192]{1,0:T(2,128)(2,1)S(1)}, bf16[128,8,1024]{2,1,0:T(8,128)(2,1)S(1)}, bf16[128,8,1024]{2,1,0:T(8,1...) custom-call(s32[16]{0:T(128)S(1)} %copy-done.6, bf16[8,24,128]{2,1,0:T(8,128)(2,1)S(1)} %get-tuple-element.94.q_ref, ...), custom_call_target="tpu_custom_call" | custom-call | tf_op jit(solution)/shard_map/exchange/pallas_call | solution.py:743
  117.3 0.0 copy-done.4
  117.3 0.0 copy-done.5
  117.3 0.0 copy-done.7
  117.3 2.1 %conditional.1 = (bf16[1,8192]{1,0:T(2,128)(2,1)}, bf16[1,2,8192]{2,1,0:T(2,128)(2,1)}, bf16[1024,1024]{1,0:T(8,128)(2,1)}, bf16[1024,1024]{1,0:T(8,128)(2,1)}, s32[128]{0:T(128)}) conditional(s32[]{:T(128)} %bitcast.14, (bf16[128,8,1024]{2,1,0:T(8,128)(2,1)S(1)}, bf16[128,8,1024]{2,1,0:T(8,128)(2,1)S(1)}, bf16[1,8192]{1,0:T(2,128)(2,1)S(1)}, ...), branch_computations={%region_0.0_spmd, %region_1.0_spmd} | conditional | bytes 40 | solution.py:884
  117.4 2.1 %write.4 = (bf16[128,8,1024]{2,1,0:T(8,128)(2,1)}, bf16[128,8,1024]{2,1,0:T(8,128)(2,1)}, bf16[1,8192]{1,0:T(2,128)(2,1)}, bf16[2,8192]{1,0:T(2,128)(2,1)}, s32[1,128]{1,0:T(1,128)}) custom-call(bf16[128,8,1024]{2,1,0:T(8,128)(2,1)S(1)} %get-tuple-element.53.k_in, bf16[128,8,1024]{2,1,0:T(8,128)(2,1)S(1)} %get-tuple-element.54.v_in, ...), custom_call_target="tpu_custom_call" | custom-call | tf_op jit(solution)/shard_map/cond/branch_0_fun/write/pallas_call | solution.py:845
Async XLA Ops:
  0.6 5.3 %copy-start.6 = (s32[16]{0:T(128)S(1)}, s32[16]{0:T(128)}, u32[]{:S(2)}) copy-start(s32[16]{0:T(128)} %counts.3) | copy-start | bytes 196
  0.6 5.3 %copy-start.3 = (bf16[512,1024]{1,0:T(8,128)(2,1)S(1)}, bf16[512,1024]{1,0:T(8,128)(2,1)}, u32[]{:S(2)}) copy-start(bf16[512,1024]{1,0:T(8,128)(2,1)} %cv_hbm.1) | copy-start | bytes 3145732
  0.7 5.3 %copy-start.2 = (bf16[512,1024]{1,0:T(8,128)(2,1)S(1)}, bf16[512,1024]{1,0:T(8,128)(2,1)}, u32[]{:S(2)}) copy-start(bf16[512,1024]{1,0:T(8,128)(2,1)} %ck_hbm.1) | copy-start | bytes 3145732
  0.7 5.3 %copy-start.1 = (bf16[1,2,1024]{2,1,0:T(2,128)(2,1)S(1)}, bf16[1,2,1024]{2,1,0:T(2,128)(2,1)}, u32[]{:S(2)}) copy-start(bf16[1,2,1024]{2,1,0:T(2,128)(2,1)} %param.18) | copy-start | bytes 12292
  0.7 5.3 %copy-start = (bf16[1,2,1024]{2,1,0:T(2,128)(2,1)S(1)}, bf16[1,2,1024]{2,1,0:T(2,128)(2,1)}, u32[]{:S(2)}) copy-start(bf16[1,2,1024]{2,1,0:T(2,128)(2,1)} %param.17) | copy-start | bytes 12292
  6.0 111.4 %copy-start.4 = (bf16[1,8192]{1,0:T(2,128)(2,1)S(1)}, bf16[1,8192]{1,0:T(2,128)(2,1)}, u32[]{:S(2)}) copy-start(bf16[1,8192]{1,0:T(2,128)(2,1)} %pq.1) | copy-start | bytes 49156
  6.0 111.3 %copy-start.5 = (bf16[1,2,8192]{2,1,0:T(2,128)(2,1)S(1)}, bf16[1,2,8192]{2,1,0:T(2,128)(2,1)}, u32[]{:S(2)}) copy-start(bf16[1,2,8192]{2,1,0:T(2,128)(2,1)} %param.16) | copy-start | bytes 98308
  6.0 111.3 %copy-start.7 = (s32[64,1]{0,1:T(1,128)S(1)}, s32[64,1]{0,1:T(1,128)}, u32[]{:S(2)}) copy-start(s32[64,1]{0,1:T(1,128)} %param.15) | copy-start | bytes 772

commit v2 on v1

--- a/solution.py
+++ b/solution.py
@@ -303,26 +303,30 @@
 
     if split:
         pieces = pieces_of(parts)
-        mine_near = my_z == 1 + half
+        inner = my_z == 1 + half
         other = (1 - half) * 2
+        by_inner, by_outer = half, 1 - half
+        keys_at, values_at = range(parts), range(parts, 2 * parts)
         HEAD, TAIL = 0, 1
+        INNER, OUTER = 0, 1
+        lands = lands[: len(pieces)], lands[len(pieces) :]
         spans = (pl.ds(0, dense - tail), pl.ds(dense - tail, tail))
 
-        def cross(piece, end, zi):
+        def cross(piece, end, side):
             kind, col, width = pieces[piece]
             src = mk_ref if kind == KEYS else mv_ref
             return pltpu.make_async_remote_copy(
                 src_ref=src.at[spans[end], :, pl.ds(col, width)],
-                dst_ref=lands[piece].at[zi, spans[end]],
-                send_sem=cross_send.at[piece, end], recv_sem=cross_recv.at[piece, end, zi],
+                dst_ref=lands[side][piece].at[spans[end]],
+                send_sem=cross_send.at[piece, end], recv_sem=cross_recv.at[piece, end, side],
                 device_id={"seq": (2 - half) * 4 + plane}, device_id_type=MESH,
             )
 
-        def hand(piece, zi):
-            buf = lands[piece]
+        def hand(piece, side):
+            buf = lands[side][piece]
             return pltpu.make_async_remote_copy(
-                src_ref=buf.at[zi, spans[TAIL]], dst_ref=buf.at[zi, pl.ds(0, tail)],
-                send_sem=pass_send.at[piece, zi], recv_sem=pass_recv.at[piece, zi],
+                src_ref=buf.at[spans[TAIL]], dst_ref=buf.at[pl.ds(0, tail)],
+                send_sem=pass_send.at[piece, side], recv_sem=pass_recv.at[piece, side],
                 device_id={"seq": 3 * half * 4 + plane}, device_id_type=MESH,
             )
 
@@ -338,51 +342,43 @@
                 device_id={"seq": my_z * 4 + to}, device_id_type=MESH,
             )
 
-        def launch(piece, end):
-            cross(piece, end, my_z % 2).start()
-
-        def pass_on(piece):
-            @pl.when(mine_near)
+        def launch(items, side):
+            for item in items:
+                cross(*item, side).start()
+
+        def pass_on(numbers, side):
+            @pl.when(inner)
             def _():
-                for zi in range(2):
-                    cross(piece, TAIL, zi).wait_recv()
-                    hand(piece, zi).start()
-
-        def unpack(piece):
+                for piece in numbers:
+                    cross(piece, TAIL, side).wait_recv()
+                    hand(piece, side).start()
+
+        def unpack(piece, side, near):
             kind, col, width = pieces[piece]
-            buf = lands[piece]
+            buf = lands[side][piece]
             out = fan_k if kind == KEYS else fan_v
             keep = store_k if kind == KEYS else store_v
             cols = pl.ds(col, width)
-
-            @pl.when(mine_near)
-            def _():
-                for zi in range(2):
-                    cross(piece, HEAD, zi).wait_recv()
-
-            @pl.when(jnp.logical_not(mine_near))
-            def _():
-                for zi in range(2):
-                    hand(piece, zi).wait_recv()
-
-            for zi in range(2):
-                shard = (other + zi) * 4 + plane
-
-                def page_at(to, k):
-                    at = meta_s[shard, ROUTE, to * cap + k]
-                    there = jnp.full((PAGE, width), at, jnp.int32) >= 0
-                    return jnp.where(
-                        there, buf[zi, jnp.maximum(at, 0)], jnp.zeros((), buf.dtype)
-                    )
-
-                def send(to):
-                    for k in range(cap):
-                        out[zi, to, k, :, cols] = page_at(to, k)
-                    fan(piece, zi, to, plane).start()
-
-                each(4, plane, send)
+            if near:
+                cross(piece, HEAD, side).wait_recv()
+            else:
+                hand(piece, side).wait_recv()
+            zi = by_inner if side == INNER else by_outer
+            shard = (other + zi) * 4 + plane
+
+            def page_at(to, k):
+                at = meta_s[shard, ROUTE, to * cap + k]
+                there = jnp.full((PAGE, width), at, jnp.int32) >= 0
+                return jnp.where(there, buf[jnp.maximum(at, 0)], jnp.zeros((), buf.dtype))
+
+            def send(to):
                 for k in range(cap):
-                    keep[shard * cap + k, :, cols] = page_at(plane, k)
+                    out[zi, to, k, :, cols] = page_at(to, k)
+                fan(piece, zi, to, plane).start()
+
+            each(4, plane, send)
+            for k in range(cap):
+                keep[shard * cap + k, :, cols] = page_at(plane, k)
 
     each(depth, my_z, lambda z: row(QROW, z).start())
     own_row(QROW).start()
@@ -390,18 +386,28 @@
     for kind in (META, KEYS, VALUES):
         own_page(kind).start()
 
+    if split:
+        order = [(p, TAIL) for p in range(2 * parts)] + [(p, HEAD) for p in range(2 * parts)]
+
+        @pl.when(inner)
+        def _():
+            launch(order[:-parts], INNER)
+
     def start_pages(peer):
         page(KEYS, peer).start()
         page(VALUES, peer).start()
 
+    own_row(QROW).wait()
+    each(depth, my_z, lambda z: row(QROW, z, True).wait_recv())
+    own_page(META).wait()
+    each(n, me, lambda peer: page(META, peer, True).wait_recv())
     if split:
         first = half * 2
         other_z = first + (1 - my_z % 2)
-        order = [(p, TAIL) for p in range(len(pieces))] + [(p, HEAD) for p in range(len(pieces))]
-        late = [(p, HEAD) for p in range(parts, 2 * parts)]
-        for item in order:
-            if item not in late:
-                launch(*item)
+        @pl.when(jnp.logical_not(inner))
+        def _():
+            launch(order[:parts], OUTER)
+
         start_pages(other_z * 4 + plane)
         start_pages(other_z * 4 + my_y * 2 + (1 - my_c))
     else:
@@ -417,17 +423,16 @@
 
         lax.fori_loop(0, depth, near, 0)
 
-    own_row(QROW).wait()
-    each(depth, my_z, lambda z: row(QROW, z, True).wait_recv())
     q_y_out = qbuf.at[:, rows_of((my_c * 2 + my_y) * depth, depth), :]
     q_y_in = qbuf.at[:, rows_of((my_c * 2 + 1 - my_y) * depth, depth), :]
     pair(0, q_y_out, q_y_out, across).start()
+    if split:
+        start_pages(my_z * 4 + (1 - my_y) * 2 + my_c)
+        start_pages(my_z * 4 + (1 - my_y) * 2 + (1 - my_c))
     pair(0, q_y_out, q_y_in, across).wait_recv()
     q_c_out = qbuf.at[:, rows_of(my_c * 2 * depth, 2 * depth), :]
     q_c_in = qbuf.at[:, rows_of((1 - my_c) * 2 * depth, 2 * depth), :]
     pair(1, q_c_out, q_c_out, sibling).start()
-    own_page(META).wait()
-    each(n, me, lambda peer: page(META, peer, True).wait_recv())
     table = pltpu.make_async_copy(meta_out, meta_s, local.at[8])
     table.start()
     if split:
@@ -469,12 +474,11 @@
         start_pages(z * 4 + (1 - my_y) * 2 + (1 - my_c))
         return 0
 
-    if split:
-        start_pages(other_z * 4 + (1 - my_y) * 2 + my_c)
-        start_pages(other_z * 4 + (1 - my_y) * 2 + (1 - my_c))
-    else:
+    if not split:
         far(0, 0)
 
+    if split:
+        pass_on(keys_at, INNER)
     lane = lax.broadcasted_iota(jnp.int32, (chunk, LANES), 1)
     keys = ck_ref.shape[0]
 
@@ -531,9 +535,6 @@
     part1s = pair(3, stat.at[rows_of(give, 2 * depth), :], got1s, sibling)
     part1s.start()
     part1.start()
-    if split:
-        for piece in range(parts):
-            pass_on(piece)
     part1s.wait_recv()
     part1.wait_recv()
     merge(obuf, stat, my_c * 2 * depth, got1, got1s, obuf1, stat1)
@@ -543,6 +544,9 @@
     part2s.start()
     part2.start()
     start_pages(sibling)
+    if split:
+        pass_on(keys_at, OUTER)
+        pass_on(values_at, INNER)
 
     own_lane = lax.broadcasted_iota(jnp.int32, (ROWS, LANES), 1)
     own_place = lax.broadcasted_iota(jnp.int32, (ROWS, LANES), 0)
@@ -568,14 +572,12 @@
     own_row(PART).start()
 
     if split:
-        for item in late:
-            launch(*item)
-        start_pages(my_z * 4 + (1 - my_y) * 2 + my_c)
-        start_pages(my_z * 4 + (1 - my_y) * 2 + (1 - my_c))
-        for piece in range(parts, 2 * parts):
-            pass_on(piece)
-        for piece in range(parts):
-            unpack(piece)
+        @pl.when(inner)
+        def _():
+            launch(order[-parts:], INNER)
+
+        start_pages(other_z * 4 + (1 - my_y) * 2 + my_c)
+        start_pages(other_z * 4 + (1 - my_y) * 2 + (1 - my_c))
     else:
         lax.fori_loop(1, depth, far, 0)
 
@@ -587,6 +589,11 @@
         row(PART, z, True).wait_recv()
 
     each(depth, my_z, wait_rows)
+
+    if split:
+        @pl.when(jnp.logical_not(inner))
+        def _():
+            launch(order[parts:], OUTER)
 
     top = functools.reduce(jnp.maximum, own_levels)
     top = lax.fori_loop(0, depth, lambda d, high: jnp.maximum(high, sbuf[d]), top)
@@ -619,8 +626,6 @@
                 dec_out[s : s + 1, at : at + HD] = result[r : r + 1]
 
     if split:
-        for piece in range(parts, 2 * parts):
-            unpack(piece)
         each(groups, my_g, lambda g: share(g, True).wait_recv())
         tables = pltpu.make_async_copy(meta_x, meta_xs, local.at[9])
         tables.start()
@@ -639,6 +644,25 @@
             over = lax.fori_loop(0, n, worse, over)
         flag_out[0] = over
 
+        @pl.when(inner)
+        def _():
+            for piece in keys_at:
+                unpack(piece, INNER, True)
+            pass_on(values_at, OUTER)
+            for piece in keys_at:
+                unpack(piece, OUTER, True)
+            for piece in values_at:
+                unpack(piece, OUTER, True)
+            for piece in values_at:
+                unpack(piece, INNER, True)
+
+        @pl.when(jnp.logical_not(inner))
+        def _():
+            for numbers in (keys_at, values_at):
+                for side in (INNER, OUTER):
+                    for piece in numbers:
+                        unpack(piece, side, False)
+
     pair(0, q_y_out, q_y_out, across).wait_send()
     pair(1, q_c_out, q_c_out, sibling).wait_send()
     for copy in (part1, part1s, part2, part2s):
@@ -663,12 +687,12 @@
         each(groups, my_g, lambda g: share(g).wait_send())
         each(n // 2, me - base, lambda i: finish(base + i))
         for item in order:
-            cross(*item, my_z % 2).wait_send()
+            cross(*item, INNER).wait_send()
         for piece in range(2 * parts):
-            @pl.when(mine_near)
+            @pl.when(inner)
             def _():
-                for zi in range(2):
-                    hand(piece, zi).wait_send()
+                for side in (INNER, OUTER):
+                    hand(piece, side).wait_send()
 
             for zi in range(2):
                 def settle(to):
@@ -728,7 +752,7 @@
         scratch += [
             pltpu.VMEM((groups,) + meta.shape, jnp.int32),
             pltpu.SMEM((groups,) + meta.shape, jnp.int32),
-            *[pltpu.VMEM((2, dense, PAGE, w), pk.dtype) for _, _, w in pieces_of(parts_count)],
+            *[pltpu.VMEM((dense, PAGE, w), pk.dtype) for _, _, w in pieces_of(parts_count) * 2],
             pltpu.VMEM((2, 4, cap, PAGE, KVD), pk.dtype),
             pltpu.VMEM((2, 4, cap, PAGE, KVD), pv.dtype),
             pltpu.SemaphoreType.DMA((groups,)),

time: 120 us -> 111 us (0.925)
  Pallas kernels: 117 us -> 109 us
    pallas_call x1, Pallas kernels: 111 us -> 101 us  [main(): pl.pallas_call(functools.partial(main_kernel, n, cap, chunk, split, dense...]
where the time goes in v2:
time: 111 us
  Pallas kernels  109 us (98%)
  between operations  2.19 us (2%)
    pallas_call x1, Pallas kernels, main(): pl.pallas_call(functools.partial(main_kernel, n, cap, chunk, split, dense...  101 us
    pallas_call x1, Pallas kernels, prep(): pl.pallas_call(functools.partial(prep_kernel, n, cap, page_slots, split,...  5.58 us

profile of v2, /device:TPU:1, one launch (start us, length us, event | category | flops | bytes accessed | tf_op | source)
XLA Modules:
  0.0 111.0 jit_solution(13572651600297472795)
XLA Ops:
  0.6 0.0 copy-start.6
  0.6 0.0 copy-start.3
  0.7 0.0 copy-start.2
  0.7 0.0 copy-start.1
  0.7 0.0 copy-start
  1.5 5.6 %prep.4 = (bf16[64,8,1024]{2,1,0:T(8,128)(2,1)S(1)}, bf16[64,8,1024]{2,1,0:T(8,128)(2,1)S(1)}, bf16[44,8,1024]{2,1,0:T(8,128)(2,1)S(1)}, bf16[44,8,1024]{2,1,0:T...) custom-call(s32[64]{0:T(128)} %bitcast.23, s32[16]{0:T(128)} %counts.3, s32[1]{0:T(128)S(6)} %copy.24.context, ...), custom_call_target="tpu_custom_call" | custom-call | tf_op jit(solution)/shard_map/prep/pallas_call | solution.py:182
  7.1 0.0 copy-done.6
  7.1 0.0 copy-done.3
  7.1 0.0 copy-done.2
  7.1 0.0 copy-done.1
  7.1 0.0 copy-done
  7.1 0.0 copy-start.4
  7.1 0.0 copy-start.5
  7.1 0.0 copy-start.7
  7.1 101.1 %exchange.1 = (bf16[1,8192]{1,0:T(2,128)(2,1)S(1)}, bf16[2,8192]{1,0:T(2,128)(2,1)S(1)}, bf16[128,8,1024]{2,1,0:T(8,128)(2,1)S(1)}, bf16[128,8,1024]{2,1,0:T(8,1...) custom-call(s32[16]{0:T(128)S(1)} %copy-done.6, bf16[8,24,128]{2,1,0:T(8,128)(2,1)S(1)} %get-tuple-element.94.q_ref, ...), custom_call_target="tpu_custom_call" | custom-call | tf_op jit(solution)/shard_map/exchange/pallas_call | solution.py:767
  108.9 0.0 copy-done.4
  108.9 0.0 copy-done.5
  108.9 0.0 copy-done.7
  108.9 2.1 %conditional.1 = (bf16[1,8192]{1,0:T(2,128)(2,1)}, bf16[1,2,8192]{2,1,0:T(2,128)(2,1)}, bf16[1024,1024]{1,0:T(8,128)(2,1)}, bf16[1024,1024]{1,0:T(8,128)(2,1)}, s32[128]{0:T(128)}) conditional(s32[]{:T(128)} %bitcast.14, (bf16[128,8,1024]{2,1,0:T(8,128)(2,1)S(1)}, bf16[128,8,1024]{2,1,0:T(8,128)(2,1)S(1)}, bf16[1,8192]{1,0:T(2,128)(2,1)S(1)}, ...), branch_computations={%region_0.0_spmd, %region_1.0_spmd} | conditional | bytes 40 | solution.py:908
  108.9 2.1 %write.4 = (bf16[128,8,1024]{2,1,0:T(8,128)(2,1)}, bf16[128,8,1024]{2,1,0:T(8,128)(2,1)}, bf16[1,8192]{1,0:T(2,128)(2,1)}, bf16[2,8192]{1,0:T(2,128)(2,1)}, s32[1,128]{1,0:T(1,128)}) custom-call(bf16[128,8,1024]{2,1,0:T(8,128)(2,1)S(1)} %get-tuple-element.53.k_in, bf16[128,8,1024]{2,1,0:T(8,128)(2,1)S(1)} %get-tuple-element.54.v_in, ...), custom_call_target="tpu_custom_call" | custom-call | tf_op jit(solution)/shard_map/cond/branch_0_fun/write/pallas_call | solution.py:869
Async XLA Ops:
  0.6 6.4 %copy-start.6 = (s32[16]{0:T(128)S(1)}, s32[16]{0:T(128)}, u32[]{:S(2)}) copy-start(s32[16]{0:T(128)} %counts.3) | copy-start | bytes 196
  0.6 6.4 %copy-start.3 = (bf16[512,1024]{1,0:T(8,128)(2,1)S(1)}, bf16[512,1024]{1,0:T(8,128)(2,1)}, u32[]{:S(2)}) copy-start(bf16[512,1024]{1,0:T(8,128)(2,1)} %cv_hbm.1) | copy-start | bytes 3145732
  0.7 6.4 %copy-start.2 = (bf16[512,1024]{1,0:T(8,128)(2,1)S(1)}, bf16[512,1024]{1,0:T(8,128)(2,1)}, u32[]{:S(2)}) copy-start(bf16[512,1024]{1,0:T(8,128)(2,1)} %ck_hbm.1) | copy-start | bytes 3145732
  0.7 6.4 %copy-start.1 = (bf16[1,2,1024]{2,1,0:T(2,128)(2,1)S(1)}, bf16[1,2,1024]{2,1,0:T(2,128)(2,1)}, u32[]{:S(2)}) copy-start(bf16[1,2,1024]{2,1,0:T(2,128)(2,1)} %param.18) | copy-start | bytes 12292
  0.7 6.4 %copy-start = (bf16[1,2,1024]{2,1,0:T(2,128)(2,1)S(1)}, bf16[1,2,1024]{2,1,0:T(2,128)(2,1)}, u32[]{:S(2)}) copy-start(bf16[1,2,1024]{2,1,0:T(2,128)(2,1)} %param.17) | copy-start | bytes 12292
  7.1 101.8 %copy-start.4 = (bf16[1,8192]{1,0:T(2,128)(2,1)S(1)}, bf16[1,8192]{1,0:T(2,128)(2,1)}, u32[]{:S(2)}) copy-start(bf16[1,8192]{1,0:T(2,128)(2,1)} %pq.1) | copy-start | bytes 49156
  7.1 101.8 %copy-start.5 = (bf16[1,2,8192]{2,1,0:T(2,128)(2,1)S(1)}, bf16[1,2,8192]{2,1,0:T(2,128)(2,1)}, u32[]{:S(2)}) copy-start(bf16[1,2,8192]{2,1,0:T(2,128)(2,1)} %param.16) | copy-start | bytes 98308
  7.1 101.8 %copy-start.7 = (s32[64,1]{0,1:T(1,128)S(1)}, s32[64,1]{0,1:T(1,128)}, u32[]{:S(2)}) copy-start(s32[64,1]{0,1:T(1,128)} %param.15) | copy-start | bytes 772

commit v3 on v2

--- a/solution.py
+++ b/solution.py
@@ -477,8 +477,6 @@
     if not split:
         far(0, 0)
 
-    if split:
-        pass_on(keys_at, INNER)
     lane = lax.broadcasted_iota(jnp.int32, (chunk, LANES), 1)
     keys = ck_ref.shape[0]
 
@@ -535,6 +533,8 @@
     part1s = pair(3, stat.at[rows_of(give, 2 * depth), :], got1s, sibling)
     part1s.start()
     part1.start()
+    if split:
+        pass_on(keys_at, OUTER)
     part1s.wait_recv()
     part1.wait_recv()
     merge(obuf, stat, my_c * 2 * depth, got1, got1s, obuf1, stat1)
@@ -545,8 +545,7 @@
     part2.start()
     start_pages(sibling)
     if split:
-        pass_on(keys_at, OUTER)
-        pass_on(values_at, INNER)
+        pass_on(keys_at, INNER)
 
     own_lane = lax.broadcasted_iota(jnp.int32, (ROWS, LANES), 1)
     own_place = lax.broadcasted_iota(jnp.int32, (ROWS, LANES), 0)
@@ -580,6 +579,9 @@
         start_pages(other_z * 4 + (1 - my_y) * 2 + (1 - my_c))
     else:
         lax.fori_loop(1, depth, far, 0)
+
+    if split:
+        pass_on(values_at, INNER)
 
     own_row(STAT).wait()
     own_row(PART).wait()

time: 111 us -> 100 us (0.901)
  Pallas kernels: 109 us -> 98 us
    pallas_call x1, Pallas kernels: 101 us -> 91.7 us  [main(): pl.pallas_call(functools.partial(main_kernel, n, cap, chunk, split, dense...]
    pallas_call x1, Pallas kernels: 5.58 us -> 4.26 us  [prep(): pl.pallas_call(functools.partial(prep_kernel, n, cap, page_slots, split,...]
where the time goes in v3:
time: 100 us
  Pallas kernels  98 us (98%)
  between operations  2.19 us (2%)
    pallas_call x1, Pallas kernels, main(): pl.pallas_call(functools.partial(main_kernel, n, cap, chunk, split, dense...  91.7 us
    pallas_call x1, Pallas kernels, prep(): pl.pallas_call(functools.partial(prep_kernel, n, cap, page_slots, split,...  4.26 us
    pallas_call x1, Pallas kernels, write(): pl.pallas_call(functools.partial(write_kernel, n, cap), in_specs=[vmem] *...  2.06 us

profile of v3, /device:TPU:1, one launch (start us, length us, event | category | flops | bytes accessed | tf_op | source)
XLA Modules:
  0.0 100.3 jit_solution(17384556670671899769)
XLA Ops:
  0.6 0.0 copy-start.6
  0.6 0.0 copy-start.3
  0.7 0.0 copy-start.2
  0.7 0.0 copy-start.1
  0.7 0.0 copy-start
  1.5 4.3 %prep.4 = (bf16[64,8,1024]{2,1,0:T(8,128)(2,1)S(1)}, bf16[64,8,1024]{2,1,0:T(8,128)(2,1)S(1)}, bf16[44,8,1024]{2,1,0:T(8,128)(2,1)S(1)}, bf16[44,8,1024]{2,1,0:T...) custom-call(s32[64]{0:T(128)} %bitcast.23, s32[16]{0:T(128)} %counts.3, s32[1]{0:T(128)S(6)} %copy.24.context, ...), custom_call_target="tpu_custom_call" | custom-call | tf_op jit(solution)/shard_map/prep/pallas_call | solution.py:182
  5.7 0.0 copy-done.6
  5.8 0.0 copy-done.3
  5.8 0.0 copy-done.2
  5.8 0.0 copy-done.1
  5.8 0.0 copy-done
  5.8 0.0 copy-start.4
  5.8 0.0 copy-start.5
  5.8 0.0 copy-start.7
  5.8 91.7 %exchange.1 = (bf16[1,8192]{1,0:T(2,128)(2,1)S(1)}, bf16[2,8192]{1,0:T(2,128)(2,1)S(1)}, bf16[128,8,1024]{2,1,0:T(8,128)(2,1)S(1)}, bf16[128,8,1024]{2,1,0:T(8,1...) custom-call(s32[16]{0:T(128)S(1)} %copy-done.6, bf16[8,24,128]{2,1,0:T(8,128)(2,1)S(1)} %get-tuple-element.94.q_ref, ...), custom_call_target="tpu_custom_call" | custom-call | tf_op jit(solution)/shard_map/exchange/pallas_call | solution.py:769
  98.2 0.0 copy-done.4
  98.2 0.0 copy-done.5
  98.2 0.0 copy-done.7
  98.2 2.1 %conditional.1 = (bf16[1,8192]{1,0:T(2,128)(2,1)}, bf16[1,2,8192]{2,1,0:T(2,128)(2,1)}, bf16[1024,1024]{1,0:T(8,128)(2,1)}, bf16[1024,1024]{1,0:T(8,128)(2,1)}, s32[128]{0:T(128)}) conditional(s32[]{:T(128)} %bitcast.14, (bf16[128,8,1024]{2,1,0:T(8,128)(2,1)S(1)}, bf16[128,8,1024]{2,1,0:T(8,128)(2,1)S(1)}, bf16[1,8192]{1,0:T(2,128)(2,1)S(1)}, ...), branch_computations={%region_0.0_spmd, %region_1.0_spmd} | conditional | bytes 40 | solution.py:910
  98.2 2.1 %write.4 = (bf16[128,8,1024]{2,1,0:T(8,128)(2,1)}, bf16[128,8,1024]{2,1,0:T(8,128)(2,1)}, bf16[1,8192]{1,0:T(2,128)(2,1)}, bf16[2,8192]{1,0:T(2,128)(2,1)}, s32[1,128]{1,0:T(1,128)}) custom-call(bf16[128,8,1024]{2,1,0:T(8,128)(2,1)S(1)} %get-tuple-element.53.k_in, bf16[128,8,1024]{2,1,0:T(8,128)(2,1)S(1)} %get-tuple-element.54.v_in, ...), custom_call_target="tpu_custom_call" | custom-call | tf_op jit(solution)/shard_map/cond/branch_0_fun/write/pallas_call | solution.py:871
Async XLA Ops:
  0.6 5.1 %copy-start.6 = (s32[16]{0:T(128)S(1)}, s32[16]{0:T(128)}, u32[]{:S(2)}) copy-start(s32[16]{0:T(128)} %counts.3) | copy-start | bytes 196
  0.6 5.1 %copy-start.3 = (bf16[512,1024]{1,0:T(8,128)(2,1)S(1)}, bf16[512,1024]{1,0:T(8,128)(2,1)}, u32[]{:S(2)}) copy-start(bf16[512,1024]{1,0:T(8,128)(2,1)} %cv_hbm.1) | copy-start | bytes 3145732
  0.7 5.1 %copy-start.2 = (bf16[512,1024]{1,0:T(8,128)(2,1)S(1)}, bf16[512,1024]{1,0:T(8,128)(2,1)}, u32[]{:S(2)}) copy-start(bf16[512,1024]{1,0:T(8,128)(2,1)} %ck_hbm.1) | copy-start | bytes 3145732
  0.7 5.1 %copy-start.1 = (bf16[1,2,1024]{2,1,0:T(2,128)(2,1)S(1)}, bf16[1,2,1024]{2,1,0:T(2,128)(2,1)}, u32[]{:S(2)}) copy-start(bf16[1,2,1024]{2,1,0:T(2,128)(2,1)} %param.18) | copy-start | bytes 12292
  0.7 5.1 %copy-start = (bf16[1,2,1024]{2,1,0:T(2,128)(2,1)S(1)}, bf16[1,2,1024]{2,1,0:T(2,128)(2,1)}, u32[]{:S(2)}) copy-start(bf16[1,2,1024]{2,1,0:T(2,128)(2,1)} %param.17) | copy-start | bytes 12292
  5.8 92.4 %copy-start.4 = (bf16[1,8192]{1,0:T(2,128)(2,1)S(1)}, bf16[1,8192]{1,0:T(2,128)(2,1)}, u32[]{:S(2)}) copy-start(bf16[1,8192]{1,0:T(2,128)(2,1)} %pq.1) | copy-start | bytes 49156
  5.8 92.4 %copy-start.5 = (bf16[1,2,8192]{2,1,0:T(2,128)(2,1)S(1)}, bf16[1,2,8192]{2,1,0:T(2,128)(2,1)}, u32[]{:S(2)}) copy-start(bf16[1,2,8192]{2,1,0:T(2,128)(2,1)} %param.16) | copy-start | bytes 98308
  5.8 92.4 %copy-start.7 = (s32[64,1]{0,1:T(1,128)S(1)}, s32[64,1]{0,1:T(1,128)}, u32[]{:S(2)}) copy-start(s32[64,1]{0,1:T(1,128)} %param.15) | copy-start | bytes 772
